TPU v7x, 32 devices: a whole 2x2x4 slice. The times are simulated.
32 devices in a mesh: col: 32 (over z, y, x, core).
Axes of the slice: x: 2, y: 2, z: 4, core: 2. Of those that a mesh axis runs over, the one named last changes fastest.
Arguments:
- a_band: float32 [1536, 24576], P(None, 'col'), may hold values from -6 to 6
- b_band: float32 [1536, 24576], P(None, 'col'), may hold values from -6 to 6
- z_band: float32 [1536, 24576], P(None, 'col'), may hold values from -6 to 6
- stacked_left_factors: float32 [1536, 384], P('col'), may hold values from -0.3125 to 0.3125
- right_factors: float32 [1536, 384], P('col'), may hold values from -0.3125 to 0.3125
- starts: int32 [4], replicated, may hold values from 512 to 23680, as said below
Outputs:
- a_out: float32 [1536, 24576], P(None, 'col')
- b_out: float32 [1536, 24576], P(None, 'col')
- z_out: float32 [1536, 24576], P(None, 'col')
Inputs may be any that keep to these rules, and one draw needn't show every extreme that they name: `starts`: Increasing; each a multiple of 128; each window's columns s to s + 383 cross exactly one border between slabs of 768 columns, and different windows cross different borders.
All inputs are finite; a program needn't handle non-finite values.
Results may differ from a plain program's by a relative error of at most 0.0001.
Values sent between devices are 32-bit elements; how exact they have to be, the bound alone decides.
A program may use at most 448 MiB of HBM per device.

v0:
```python
import functools

import jax
import jax.numpy as jnp
from jax import lax
from jax.experimental import pallas as pl
from jax.experimental.pallas import tpu as pltpu
from jax.sharding import PartitionSpec as P

ALIGN = 128
CORES = 2
PLANE = 4
F32 = jnp.float32
BF16 = jnp.bfloat16
VMEM_LIMIT = 60 * 1024 * 1024


def split(x):
    high = x.astype(BF16)
    return high, (x - high.astype(F32)).astype(BF16)


def mm(x, w):
    rows = x.shape[0]
    xh, xl = split(x)
    wh, wl = split(w)
    both = jnp.dot(jnp.concatenate([xh, xl], axis=0), wh, preferred_element_type=F32)
    return both[:rows] + (both[rows:] + jnp.dot(xh, wl, preferred_element_type=F32))


def borders(info, count, width, cols):
    first = info[count]
    last = first + cols
    left = (jnp.bool_(False), jnp.int32(0), jnp.int32(0))
    right = left
    for k in range(count):
        s = info[k]
        at_left = (s < first) & (first < s + width)
        at_right = (s < last) & (last < s + width)
        left = (
            left[0] | at_left,
            jnp.where(at_left, k, left[1]),
            jnp.where(at_left, s + width - first, left[2]),
        )
        right = (
            right[0] | at_right,
            jnp.where(at_right, k, right[1]),
            jnp.where(at_right, last - s, right[2]),
        )
    return first, left, right


def prep_kernel(count, width, cols, info, al, ar, bl, br, zl, zr, rights, down, up):
    wide = width - ALIGN
    _, left, right = borders(info, count, width, cols)
    for i, (lo, hi) in enumerate(((al, ar), (bl, br), (zl, zr))):
        full_left = left[0] & (left[2] == wide)
        full_right = right[0] & (right[2] == wide)

        @pl.when(full_left)
        def _():
            down[i] = mm(lo[...], rights[left[1], width - wide : width, 0:ALIGN])

        @pl.when(jnp.logical_not(full_left))
        def _():
            down[i] = lo[:, 0:ALIGN]

        @pl.when(full_right)
        def _():
            up[i] = mm(hi[...], rights[right[1], 0:wide, width - ALIGN : width])

        @pl.when(jnp.logical_not(full_right))
        def _():
            up[i] = hi[:, wide - ALIGN : wide]


def main_kernel(count, width, cols, info, a, b, z, left_factor, rights, a_out, b_out, z_out):
    wide = width - ALIGN
    j = pl.program_id(0)
    first, left, right = borders(info, count, width, cols)
    threshold = info[j] - first

    @pl.when(threshold < cols)
    def _():
        turned = left_factor[...].T
        keep = lax.broadcasted_iota(jnp.int32, (width, cols), 1) >= threshold
        for src, dst in ((a, a_out), (b, b_out)):
            x = src[...]
            dst[...] = jnp.where(keep, mm(turned, x), x)

    @pl.when(threshold >= cols)
    def _():
        a_out[...] = a[...]
        b_out[...] = b[...]

    z_out[...] = z[...]
    for dst, always in ((a_out, False), (b_out, False), (z_out, True)):
        on_left = left[0] if always else left[0] & (j <= left[1])
        on_right = right[0] if always else right[0] & (j <= right[1])

        @pl.when(on_left & (left[2] == wide))
        def _():
            dst[:, 0:wide] = mm(dst[:, 0:wide], rights[left[1], width - wide : width, width - wide : width])

        @pl.when(on_left & (left[2] == ALIGN))
        def _():
            dst[:, 0:ALIGN] = mm(dst[:, 0:ALIGN], rights[left[1], width - ALIGN : width, width - ALIGN : width])

        @pl.when(on_right & (right[2] == wide))
        def _():
            dst[:, cols - wide : cols] = mm(dst[:, cols - wide : cols], rights[right[1], 0:wide, 0:wide])

        @pl.when(on_right & (right[2] == ALIGN))
        def _():
            dst[:, cols - ALIGN : cols] = mm(dst[:, cols - ALIGN : cols], rights[right[1], 0:ALIGN, 0:ALIGN])


def edge_of(count, width, cols, upto, step, info):
    _, left, right = borders(info, count, width, cols)
    side = step // count
    j = lax.rem(step, count)
    low_last, high_last = (left[1], right[1]) if upto else (count - 1, count - 1)
    low = jnp.where(left[0], jnp.where(side == 0, jnp.minimum(j, low_last), low_last), 0)
    high = jnp.where(side == 0, 0, jnp.minimum(j, high_last))
    at_high = right[0] & ((side == 1) | jnp.logical_not(left[0]))
    return jnp.where(at_high, high, low), at_high.astype(jnp.int32)


def finish_kernel(count, width, cols, info, a, b, z, from_left, from_right, left_factor, rights, a_out, b_out, z_out):
    wide = width - ALIGN
    step = pl.program_id(0)
    side = step // count
    j = lax.rem(step, count)
    _, left, right = borders(info, count, width, cols)
    for upto, group in ((True, ((a, a_out), (b, b_out))), (False, ((z, z_out),))):
        now = edge_of(count, width, cols, upto, step, info)
        then = edge_of(count, width, cols, upto, jnp.maximum(step - 1, 0), info)

        @pl.when((step == 0) | (now[0] != then[0]) | (now[1] != then[1]))
        def _():
            for src, dst in group:
                dst[...] = src[...]

    def add(received, at, rows_of, near, far, window):
        present, k, here = window
        for i, dst in enumerate((a_out, b_out, z_out)):
            wanted = present & (side == at)
            if i < 2:
                wanted = wanted & (j <= k)

            @pl.when(wanted)
            def _():
                g = received[i]
                if i < 2:
                    g = mm(left_factor[...].T, g)

                @pl.when(here == wide)
                def _():
                    dst[...] = dst[...] + mm(g, rights[k, rows_of : rows_of + ALIGN, far : far + wide])

                @pl.when(here == ALIGN)
                def _():
                    dst[:, near : near + ALIGN] = dst[:, near : near + ALIGN] + g

    add(from_left, 0, 0, 0, width - wide, left)
    add(from_right, 1, width - ALIGN, wide - ALIGN, 0, right)


def gather_kernel(n, rights, lefts, all_rights, all_lefts, own_sem, out_sems, plane_sems, core_sems, recv_sems):
    me = lax.axis_index("col")
    core = lax.rem(me, CORES)
    chip = me // CORES
    place = lax.rem(chip, PLANE)
    outer = chip // PLANE
    outers = n // (CORES * PLANE)
    pair = ((rights, all_rights), (lefts, all_lefts))

    def device(o, p, c):
        return (lax.rem(o, outers) * PLANE + lax.rem(p, PLANE)) * CORES + c

    far = [device(outer + d, place, core) for d in range(1, outers)]
    near = [device(outer, place + q, core) for q in range(1, PLANE)]
    twin = device(outer, place, 1 - core)

    barrier = pltpu.get_barrier_semaphore()
    for peer in far + near + [twin]:
        pl.semaphore_signal(barrier, inc=1, device_id=(peer,), device_id_type=pl.DeviceIdType.MESH)
    pl.semaphore_wait(barrier, len(far) + len(near) + 1)

    started = []

    def send(which, source, piece, send_sem, target):
        copy = pltpu.make_async_remote_copy(
            src_ref=source,
            dst_ref=pair[which][1].at[piece],
            send_sem=send_sem,
            recv_sem=recv_sems.at[which, piece],
            device_id=(target,),
            device_id_type=pl.DeviceIdType.MESH,
        )
        copy.start()
        started.append(copy)

    def arrived(which, piece):
        here = pair[which][1].at[piece]
        pltpu.make_async_copy(here, here, recv_sems.at[which, piece]).wait()

    def spread(which, source, piece, d):
        for q in range(1, PLANE):
            send(which, source, piece, plane_sems.at[which, d, q - 1], near[q - 1])
        send(which, source, piece, core_sems.at[which, d, 0], twin)

    own = []
    for which, (mine, everyone) in enumerate(pair):
        for d in range(1, outers):
            send(which, mine, me, out_sems.at[which, d - 1], far[d - 1])
        spread(which, mine, me, 0)
        own.append(pltpu.make_async_copy(mine, everyone.at[me], own_sem.at[which]))
        own[-1].start()
    for which, (_, everyone) in enumerate(pair):
        for d in range(1, outers):
            piece = device(outer + outers - d, place, core)
            arrived(which, piece)
            spread(which, everyone.at[piece], piece, d)
    for which, (_, everyone) in enumerate(pair):
        for d in range(outers):
            for q in range(1, PLANE):
                piece = device(outer + outers - d, place + PLANE - q, core)
                arrived(which, piece)
                send(which, everyone.at[piece], piece, core_sems.at[which, d, q], twin)
    for which in range(2):
        for d in range(outers):
            for q in range(PLANE):
                arrived(which, device(outer + outers - d, place + PLANE - q, 1 - core))
    for copy in started:
        copy.wait_send()
    for copy in own:
        copy.wait()


def gathered(rights, lefts, n):
    pieces = jax.ShapeDtypeStruct((n,) + rights.shape, F32)
    outers = n // (CORES * PLANE)
    vmem = pl.BlockSpec(memory_space=pltpu.VMEM)
    anywhere = pl.BlockSpec(memory_space=pl.ANY)
    dma = pltpu.SemaphoreType.DMA
    return pl.pallas_call(
        functools.partial(gather_kernel, n),
        out_shape=(pieces, pieces),
        in_specs=[vmem, vmem],
        out_specs=(anywhere, anywhere),
        scratch_shapes=[
            dma((2,)),
            dma((2, max(outers - 1, 1))),
            dma((2, outers, PLANE - 1)),
            dma((2, outers, PLANE)),
            dma((2, n)),
        ],
        compiler_params=pltpu.CompilerParams(collective_id=0, has_side_effects=True),
        name="gather",
    )(rights, lefts)


def local(n, a_band, b_band, z_band, stacked_left_factors, right_factors, starts):
    width = stacked_left_factors.shape[1]
    count = starts.shape[0]
    rows, cols = a_band.shape
    wide = width - ALIGN
    rights, lefts = gathered(right_factors, stacked_left_factors, n)
    rights = rights.reshape(count, width, width)
    lefts = lefts.reshape(count, width, width)
    first = (lax.axis_index("col") * cols).astype(jnp.int32)
    info = jnp.concatenate([starts, first[None]])
    far = cols // wide - 1
    params = pltpu.CompilerParams(vmem_limit_bytes=VMEM_LIMIT)
    all_rights = pl.BlockSpec((count, width, width), lambda *_: (0, 0, 0), pipeline_mode=pl.Buffered(1))
    strip = jax.ShapeDtypeStruct((3, rows, ALIGN), F32)
    low = pl.BlockSpec((width, wide), lambda j, s: (j, 0))
    high = pl.BlockSpec((width, wide), lambda j, s: (j, far))
    strip_spec = pl.BlockSpec((3, width, ALIGN), lambda j, *_: (0, j, 0))
    down, up = pl.pallas_call(
        functools.partial(prep_kernel, count, width, cols),
        out_shape=(strip, strip),
        grid_spec=pltpu.PrefetchScalarGridSpec(
            num_scalar_prefetch=1,
            grid=(count,),
            in_specs=[low, high, low, high, low, high, all_rights],
            out_specs=[strip_spec, strip_spec],
        ),
        compiler_params=params,
        name="prep",
    )(info, a_band, a_band, b_band, b_band, z_band, z_band, rights)
    whole = jax.ShapeDtypeStruct((rows, cols), F32)
    slab = pl.BlockSpec((width, cols), lambda j, s: (j, 0))
    one_left = pl.BlockSpec((None, width, width), lambda j, *_: (j, 0, 0))
    main = pl.pallas_call(
        functools.partial(main_kernel, count, width, cols),
        out_shape=(whole, whole, whole),
        grid_spec=pltpu.PrefetchScalarGridSpec(
            num_scalar_prefetch=1,
            grid=(count,),
            in_specs=[slab, slab, slab, one_left, all_rights],
            out_specs=[slab, slab, slab],
        ),
        compiler_params=params,
        cost_estimate=pl.CostEstimate(
            flops=20 * rows * cols * width, bytes_accessed=24 * rows * cols, transcendentals=0
        ),
        name="main",
    )

    def exchange(odd, even, up, down, *operands):
        wanted = {1: odd, 0: even}
        pairs = [
            (i, i + 1)
            for i in range(n - 1)
            if (i + 1) % CORES or wanted[(i + 1) // CORES % 2]
        ]
        from_left = lax.ppermute(up, "col", pairs)
        from_right = lax.ppermute(down, "col", [(j, i) for i, j in pairs])
        return (from_left, from_right) + tuple(main(*operands))

    crossed = (starts + (width - 1)) // cols
    chip_border = crossed % CORES == 0
    odd_ones = jnp.any(chip_border & (crossed // CORES % 2 == 1))
    even_ones = jnp.any(chip_border & (crossed // CORES % 2 == 0))
    from_left, from_right, a_mid, b_mid, z_mid = lax.switch(
        odd_ones.astype(jnp.int32) + 2 * even_ones.astype(jnp.int32),
        [functools.partial(exchange, odd, even) for even in (False, True) for odd in (False, True)],
        up, down, info, a_band, b_band, z_band, lefts, rights,
    )

    def edge(upto):
        def index(step, info):
            block, at_high = edge_of(count, width, cols, upto, step, info)
            return block, at_high * far

        return pl.BlockSpec((width, wide), index)

    edges = [edge(True), edge(True), edge(False)]
    strip_of = pl.BlockSpec((3, width, ALIGN), lambda step, s: (0, lax.rem(step, count), 0))
    left_of = pl.BlockSpec((None, width, width), lambda step, s: (lax.rem(step, count), 0, 0))
    return pl.pallas_call(
        functools.partial(finish_kernel, count, width, cols),
        out_shape=(whole, whole, whole),
        grid_spec=pltpu.PrefetchScalarGridSpec(
            num_scalar_prefetch=1,
            grid=(2 * count,),
            in_specs=edges + [strip_of, strip_of, left_of, all_rights],
            out_specs=edges,
        ),
        input_output_aliases={1: 0, 2: 1, 3: 2},
        compiler_params=params,
        name="finish",
    )(info, a_mid, b_mid, z_mid, from_left, from_right, lefts, rights)


def solution(mesh):
    placed = (P(None, "col"), P(None, "col"), P(None, "col"), P("col", None), P("col", None), P())
    return jax.shard_map(
        functools.partial(local, mesh.shape["col"]),
        mesh=mesh,
        in_specs=placed,
        out_specs=(P(None, "col"), P(None, "col"), P(None, "col")),
        check_vma=False,
    )
```

profile of v0, /device:TPU:15, one launch (start us, length us, event | category | flops | bytes accessed | tf_op | source)
XLA Modules:
  0.0 93.1 jit_solution(18445413203158605328)
XLA Ops:
  0.6 0.7 pad_add_fusion.info
  1.4 0.7 and_select_fusion
  2.0 0.6 and_reduce_fusion
  4.0 32.9 %gather.1 = (f32[32,48,384]{2,1,0:T(8,128)S(1)}, f32[32,48,384]{2,1,0:T(8,128)}) custom-call(f32[48,384]{1,0:T(8,128)} %rights.1, f32[48,384]{1,0:T(8,128)} %lefts.1), custom_call_target="tpu_custom_call" | custom-call | tf_op jit(solution)/shard_map/gather/pallas_call | solution.py:247
  36.9 6.7 %prep.1 = (f32[3,1536,128]{2,1,0:T(8,128)}, f32[3,1536,128]{2,1,0:T(8,128)}) custom-call(s32[5]{0:T(128)S(1)} %pad_add_fusion.info, f32[1536,768]{1,0:T(8,128)} %ar.1, f32[1536,768]{1,0:T(8,128)} %ar.1, f32[1536,768]{1,0:T(8,128)} %br.1, f32[1536,768]{1,0:T(8,128)} %br.1, f32[1536,768]{1,0:T(8,128)} %zr.1, f32[1536,768]{1,0:T(8,128)} %zr.1, ...), custom_call_target="tpu_custom_call" | custom-call | tf_op jit(solution)/shard_map/prep/pallas_call | solution.py:281
  43.7 37.7 %conditional.1 = (f32[3,1536,128]{2,1,0:T(8,128)}, f32[3,1536,128]{2,1,0:T(8,128)}, f32[1536,768]{1,0:T(8,128)}, f32[1536,768]{1,0:T(8,128)}, f32[1536,768]{1,0:T(8,128)}) conditional(s32[]{:T(128)} %clamp.3, (f32[3,1536,128]{2,1,0:T(8,128)}, f32[3,1536,128]{2,1,0:T(8,128)}, s32[5]{0:T(128)S(1)}, ...), branch_computations={%region_2.3_spmd, %region_3.4_spmd, %region_4.5_spmd, %region_5.6_... | conditional | flops 9059696640 | bytes 47186040 | solution.py:327
  43.7 5.4 %collective-permute-start.4 = (f32[3,1536,128]{2,1,0:T(8,128)}, f32[3,1536,128]{2,1,0:T(8,128)}, u32[]{:S(2)}, u32[]{:S(2)}) collective-permute-start(f32[3,1536,128]{2,1,0:T(8,128)} %get-tuple-element.86), channel_id=1, source_target_pairs={{0,1},{2,3},{3,4},{4,5},{6,7},{7,8},{8,9},{10,11},{11,12},{12,13},... | collective-permute-start | bytes 7077896 | tf_op jit(solution)/shard_map/cond/branch_2_fun/ppermute | solution.py:319
  49.1 2.1 %collective-permute-start.5 = (f32[3,1536,128]{2,1,0:T(8,128)}, f32[3,1536,128]{2,1,0:T(8,128)}, u32[]{:S(2)}, u32[]{:S(2)}) collective-permute-start(f32[3,1536,128]{2,1,0:T(8,128)} %get-tuple-element.87), channel_id=1, source_target_pairs={{1,0},{3,2},{4,3},{5,4},{7,6},{8,7},{9,8},{11,10},{12,11},{13,12},... | collective-permute-start | bytes 7077896 | tf_op jit(solution)/shard_map/cond/branch_2_fun/ppermute | solution.py:320
  51.2 14.7 %main.6 = (f32[1536,768]{1,0:T(8,128)}, f32[1536,768]{1,0:T(8,128)}, f32[1536,768]{1,0:T(8,128)}) custom-call(s32[5]{0:T(128)S(1)} %get-tuple-element.88.info, f32[1536,768]{1,0:T(8,128)} %get-tuple-element.89.a, f32[1536,768]{1,0:T(8,128)} %get-tuple-element.90.b, f32[1536,768]{1,0:T(8,128)} %get-tuple-element.91.z, ...), custom_call_target="tpu_custom_call" | custom-call | flops 9059696640 | bytes 28311552 | tf_op jit(solution)/shard_map/cond/branch_2_fun/main/pallas_call | solution.py:321
  65.9 9.3 %collective-permute-done.4 = f32[3,1536,128]{2,1,0:T(8,128)} collective-permute-done((f32[3,1536,128]{2,1,0:T(8,128)}, f32[3,1536,128]{2,1,0:T(8,128)}, u32[]{:S(2)}, u32[]{:S(2)}) %collective-permute-start.4) | collective-permute-done | bytes 2359328 | tf_op jit(solution)/shard_map/cond/branch_2_fun/ppermute | solution.py:319
  75.1 6.2 %collective-permute-done.5 = f32[3,1536,128]{2,1,0:T(8,128)} collective-permute-done((f32[3,1536,128]{2,1,0:T(8,128)}, f32[3,1536,128]{2,1,0:T(8,128)}, u32[]{:S(2)}, u32[]{:S(2)}) %collective-permute-start.5) | collective-permute-done | bytes 2359328 | tf_op jit(solution)/shard_map/cond/branch_2_fun/ppermute | solution.py:320
  81.3 11.7 %finish.1 = (f32[1536,768]{1,0:T(8,128)}, f32[1536,768]{1,0:T(8,128)}, f32[1536,768]{1,0:T(8,128)}) custom-call(s32[5]{0:T(128)S(1)} %pad_add_fusion.info, f32[1536,768]{1,0:T(8,128)} %get-tuple-element.124.a, f32[1536,768]{1,0:T(8,128)} %get-tuple-element.125.b, ...), custom_call_target="tpu_custom_call", output_to_operand_aliasing={{0}: (1, {}), {1}: (2, {}), {2}: (3, {})} | custom-call | tf_op jit(solution)/shard_map/finish/pallas_call | solution.py:343
Async XLA Ops:
  43.7 31.5 %collective-permute-start.4 = (f32[3,1536,128]{2,1,0:T(8,128)}, f32[3,1536,128]{2,1,0:T(8,128)}, u32[]{:S(2)}, u32[]{:S(2)}) collective-permute-start(f32[3,1536,128]{2,1,0:T(8,128)} %get-tuple-element.86), channel_id=1, source_target_pairs={{0,1},{2,3},{3,4},{4,5},{6,7},{7,8},{8,9},{10,11},{11,12},{12,13},... | collective-permute-start | bytes 7077896 | tf_op jit(solution)/shard_map/cond/branch_2_fun/ppermute | solution.py:319
  49.1 32.3 %collective-permute-start.5 = (f32[3,1536,128]{2,1,0:T(8,128)}, f32[3,1536,128]{2,1,0:T(8,128)}, u32[]{:S(2)}, u32[]{:S(2)}) collective-permute-start(f32[3,1536,128]{2,1,0:T(8,128)} %get-tuple-element.87), channel_id=1, source_target_pairs={{1,0},{3,2},{4,3},{5,4},{7,6},{8,7},{9,8},{11,10},{12,11},{13,12},... | collective-permute-start | bytes 7077896 | tf_op jit(solution)/shard_map/cond/branch_2_fun/ppermute | solution.py:320
where the time goes:
time: 93.6 us; the launch traced here: 93.1 us
  Pallas kernels  66.1 us (71%)
  waiting for transfers between devices  15.5 us (17%)
  starting transfers between devices  7.5 us (8%)
  other arithmetic  2.05 us (2%)
  between operations  1.95 us (2%)
    pallas_call x1, Pallas kernels, gathered(): pl.pallas_call(functools.partial(gather_kernel, n), out_shape=(pieces, pi...  32.9 us
    pallas_call x1, Pallas kernels, exchange(): return (from_left, from_right) + tuple(main(*operands))  14.7 us
    pallas_call x1, Pallas kernels, local(): pl.pallas_call(functools.partial(finish_kernel, count, width, cols), out_...  11.7 us
    ppermute x1, waiting for transfers between devices, exchange(): from_left = lax.ppermute(up, 'col', pairs)  9.29 us
    pallas_call x1, Pallas kernels, local(): pl.pallas_call(functools.partial(prep_kernel, count, width, cols), out_sh...  6.72 us
    ppermute x1, waiting for transfers between devices, exchange(): from_right = lax.ppermute(down, 'col', [(j, i) for i, j in pairs])  6.19 us
    ppermute x1, starting transfers between devices, exchange(): from_left = lax.ppermute(up, 'col', pairs)  5.4 us
    ppermute x1, starting transfers between devices, exchange(): from_right = lax.ppermute(down, 'col', [(j, i) for i, j in pairs])  2.1 us
  transfers between devices with their start and end apart: 2, of which 2 were waited for; matrix products, arithmetic and copies ran while one was open for 0% of the time, Pallas kernels for 16%

commit v1 on v0

--- a/solution.py
+++ b/solution.py
@@ -174,12 +174,15 @@
     outer = chip // PLANE
     outers = n // (CORES * PLANE)
     pair = ((rights, all_rights), (lefts, all_lefts))
+    beside = place + 1 - 2 * lax.rem(place, 2)
+    across = lax.rem(place + 2, PLANE)
+    diagonal = PLANE - 1 - place
 
     def device(o, p, c):
-        return (lax.rem(o, outers) * PLANE + lax.rem(p, PLANE)) * CORES + c
+        return (lax.rem(o, outers) * PLANE + p) * CORES + c
 
     far = [device(outer + d, place, core) for d in range(1, outers)]
-    near = [device(outer, place + q, core) for q in range(1, PLANE)]
+    near = [device(outer, beside, core), device(outer, across, core)]
     twin = device(outer, place, 1 - core)
 
     barrier = pltpu.get_barrier_semaphore()
@@ -204,10 +207,11 @@
     def arrived(which, piece):
         here = pair[which][1].at[piece]
         pltpu.make_async_copy(here, here, recv_sems.at[which, piece]).wait()
+        return here
 
     def spread(which, source, piece, d):
-        for q in range(1, PLANE):
-            send(which, source, piece, plane_sems.at[which, d, q - 1], near[q - 1])
+        for q in range(2):
+            send(which, source, piece, plane_sems.at[which, d, q], near[q])
         send(which, source, piece, core_sems.at[which, d, 0], twin)
 
     own = []
@@ -217,21 +221,30 @@
         spread(which, mine, me, 0)
         own.append(pltpu.make_async_copy(mine, everyone.at[me], own_sem.at[which]))
         own[-1].start()
-    for which, (_, everyone) in enumerate(pair):
+    for which in range(2):
         for d in range(1, outers):
             piece = device(outer + outers - d, place, core)
-            arrived(which, piece)
-            spread(which, everyone.at[piece], piece, d)
+            spread(which, arrived(which, piece), piece, d)
     for which, (_, everyone) in enumerate(pair):
         for d in range(outers):
-            for q in range(1, PLANE):
-                piece = device(outer + outers - d, place + PLANE - q, core)
+            origin = lax.rem(outer + outers - d, outers)
+            odd = lax.rem(origin + which, 2)
+            pieces = [device(origin, beside, core), device(origin, across, core)]
+            for piece in pieces:
                 arrived(which, piece)
-                send(which, everyone.at[piece], piece, core_sems.at[which, d, q], twin)
+            relayed = pieces[0] * (1 - odd) + pieces[1] * odd
+            target = near[1] * (1 - odd) + near[0] * odd
+            send(which, everyone.at[relayed], relayed, plane_sems.at[which, d, 2], target)
+            for q, piece in enumerate(pieces):
+                send(which, everyone.at[piece], piece, core_sems.at[which, d, 1 + q], twin)
     for which in range(2):
         for d in range(outers):
-            for q in range(PLANE):
-                arrived(which, device(outer + outers - d, place + PLANE - q, 1 - core))
+            piece = device(outer + outers - d, diagonal, core)
+            send(which, arrived(which, piece), piece, core_sems.at[which, d, 3], twin)
+    for which in range(2):
+        for d in range(outers):
+            for p in (place, beside, across, diagonal):
+                arrived(which, device(outer + outers - d, p, 1 - core))
     for copy in started:
         copy.wait_send()
     for copy in own:

time: 93.6 us -> 90.8 us (0.970)
  Pallas kernels: 66.1 us -> 64.2 us
  starting transfers between devices: 7.5 us -> 6.42 us
    pallas_call x1, Pallas kernels: 32.9 us -> 30.6 us  [gathered(): pl.pallas_call(functools.partial(gather_kernel, n), out_shape=(pieces, pi...]
    ppermute x1, starting transfers between devices: 5.4 us -> 4.32 us  [exchange(): from_left = lax.ppermute(up, 'col', pairs)]
  transfers between devices with their start and end apart: 2 -> 2, of which waited for: 2 -> 2; matrix products, arithmetic and copies ran while one was open for 0% -> 0% of each run, Pallas kernels for 16% -> 17%
where the time goes in v1:
time: 90.8 us; the launch traced here: 89.4 us
  Pallas kernels  64.2 us (71%)
  waiting for transfers between devices  14.7 us (16%)
  starting transfers between devices  6.42 us (7%)
  other arithmetic  2.05 us (2%)
  between operations  1.95 us (2%)
    pallas_call x1, Pallas kernels, gathered(): pl.pallas_call(functools.partial(gather_kernel, n), out_shape=(pieces, pi...  30.6 us
    pallas_call x1, Pallas kernels, exchange(): return (from_left, from_right) + tuple(main(*operands))  15.5 us
    pallas_call x1, Pallas kernels, local(): pl.pallas_call(functools.partial(finish_kernel, count, width, cols), out_...  11.5 us
    ppermute x1, waiting for transfers between devices, exchange(): from_left = lax.ppermute(up, 'col', pairs)  8.5 us
    pallas_call x1, Pallas kernels, local(): pl.pallas_call(functools.partial(prep_kernel, count, width, cols), out_sh...  6.72 us
    ppermute x1, waiting for transfers between devices, exchange(): from_right = lax.ppermute(down, 'col', [(j, i) for i, j in pairs])  6.19 us
    ppermute x1, starting transfers between devices, exchange(): from_left = lax.ppermute(up, 'col', pairs)  4.32 us
    ppermute x1, starting transfers between devices, exchange(): from_right = lax.ppermute(down, 'col', [(j, i) for i, j in pairs])  2.1 us
  transfers between devices with their start and end apart: 2, of which 2 were waited for; matrix products, arithmetic and copies ran while one was open for 0% of the time, Pallas kernels for 17%

profile of v1, /device:TPU:15, one launch (start us, length us, event | category | flops | bytes accessed | tf_op | source)
XLA Modules:
  0.0 89.4 jit_solution(4253616050536465004)
XLA Ops:
  0.6 0.7 pad_add_fusion.info
  1.4 0.7 and_select_fusion
  2.0 0.6 and_reduce_fusion
  4.0 30.6 %gather.1 = (f32[32,48,384]{2,1,0:T(8,128)S(1)}, f32[32,48,384]{2,1,0:T(8,128)}) custom-call(f32[48,384]{1,0:T(8,128)} %rights.1, f32[48,384]{1,0:T(8,128)} %lefts.1), custom_call_target="tpu_custom_call" | custom-call | tf_op jit(solution)/shard_map/gather/pallas_call | solution.py:260
  34.6 6.7 %prep.1 = (f32[3,1536,128]{2,1,0:T(8,128)}, f32[3,1536,128]{2,1,0:T(8,128)}) custom-call(s32[5]{0:T(128)S(1)} %pad_add_fusion.info, f32[1536,768]{1,0:T(8,128)} %ar.1, f32[1536,768]{1,0:T(8,128)} %ar.1, f32[1536,768]{1,0:T(8,128)} %br.1, f32[1536,768]{1,0:T(8,128)} %br.1, f32[1536,768]{1,0:T(8,128)} %zr.1, f32[1536,768]{1,0:T(8,128)} %zr.1, ...), custom_call_target="tpu_custom_call" | custom-call | tf_op jit(solution)/shard_map/prep/pallas_call | solution.py:294
  41.3 36.6 %conditional.1 = (f32[3,1536,128]{2,1,0:T(8,128)}, f32[3,1536,128]{2,1,0:T(8,128)}, f32[1536,768]{1,0:T(8,128)}, f32[1536,768]{1,0:T(8,128)}, f32[1536,768]{1,0:T(8,128)}) conditional(s32[]{:T(128)} %clamp.3, (f32[3,1536,128]{2,1,0:T(8,128)}, f32[3,1536,128]{2,1,0:T(8,128)}, s32[5]{0:T(128)S(1)}, ...), branch_computations={%region_2.3_spmd, %region_3.4_spmd, %region_4.5_spmd, %region_5.6_... | conditional | flops 9059696640 | bytes 47186040 | solution.py:340
  41.3 4.3 %collective-permute-start.4 = (f32[3,1536,128]{2,1,0:T(8,128)}, f32[3,1536,128]{2,1,0:T(8,128)}, u32[]{:S(2)}, u32[]{:S(2)}) collective-permute-start(f32[3,1536,128]{2,1,0:T(8,128)} %get-tuple-element.86), channel_id=1, source_target_pairs={{0,1},{2,3},{3,4},{4,5},{6,7},{7,8},{8,9},{10,11},{11,12},{12,13},... | collective-permute-start | bytes 7077896 | tf_op jit(solution)/shard_map/cond/branch_2_fun/ppermute | solution.py:332
  45.6 2.1 %collective-permute-start.5 = (f32[3,1536,128]{2,1,0:T(8,128)}, f32[3,1536,128]{2,1,0:T(8,128)}, u32[]{:S(2)}, u32[]{:S(2)}) collective-permute-start(f32[3,1536,128]{2,1,0:T(8,128)} %get-tuple-element.87), channel_id=1, source_target_pairs={{1,0},{3,2},{4,3},{5,4},{7,6},{8,7},{9,8},{11,10},{12,11},{13,12},... | collective-permute-start | bytes 7077896 | tf_op jit(solution)/shard_map/cond/branch_2_fun/ppermute | solution.py:333
  47.7 15.5 %main.6 = (f32[1536,768]{1,0:T(8,128)}, f32[1536,768]{1,0:T(8,128)}, f32[1536,768]{1,0:T(8,128)}) custom-call(s32[5]{0:T(128)S(1)} %get-tuple-element.88.info, f32[1536,768]{1,0:T(8,128)} %get-tuple-element.89.a, f32[1536,768]{1,0:T(8,128)} %get-tuple-element.90.b, f32[1536,768]{1,0:T(8,128)} %get-tuple-element.91.z, ...), custom_call_target="tpu_custom_call" | custom-call | flops 9059696640 | bytes 28311552 | tf_op jit(solution)/shard_map/cond/branch_2_fun/main/pallas_call | solution.py:334
  63.2 8.5 %collective-permute-done.4 = f32[3,1536,128]{2,1,0:T(8,128)} collective-permute-done((f32[3,1536,128]{2,1,0:T(8,128)}, f32[3,1536,128]{2,1,0:T(8,128)}, u32[]{:S(2)}, u32[]{:S(2)}) %collective-permute-start.4) | collective-permute-done | bytes 2359328 | tf_op jit(solution)/shard_map/cond/branch_2_fun/ppermute | solution.py:332
  71.7 6.2 %collective-permute-done.5 = f32[3,1536,128]{2,1,0:T(8,128)} collective-permute-done((f32[3,1536,128]{2,1,0:T(8,128)}, f32[3,1536,128]{2,1,0:T(8,128)}, u32[]{:S(2)}, u32[]{:S(2)}) %collective-permute-start.5) | collective-permute-done | bytes 2359328 | tf_op jit(solution)/shard_map/cond/branch_2_fun/ppermute | solution.py:333
  77.9 11.5 %finish.1 = (f32[1536,768]{1,0:T(8,128)}, f32[1536,768]{1,0:T(8,128)}, f32[1536,768]{1,0:T(8,128)}) custom-call(s32[5]{0:T(128)S(1)} %pad_add_fusion.info, f32[1536,768]{1,0:T(8,128)} %get-tuple-element.124.a, f32[1536,768]{1,0:T(8,128)} %get-tuple-element.125.b, ...), custom_call_target="tpu_custom_call", output_to_operand_aliasing={{0}: (1, {}), {1}: (2, {}), {2}: (3, {})} | custom-call | tf_op jit(solution)/shard_map/finish/pallas_call | solution.py:356
Async XLA Ops:
  41.3 30.4 %collective-permute-start.4 = (f32[3,1536,128]{2,1,0:T(8,128)}, f32[3,1536,128]{2,1,0:T(8,128)}, u32[]{:S(2)}, u32[]{:S(2)}) collective-permute-start(f32[3,1536,128]{2,1,0:T(8,128)} %get-tuple-element.86), channel_id=1, source_target_pairs={{0,1},{2,3},{3,4},{4,5},{6,7},{7,8},{8,9},{10,11},{11,12},{12,13},... | collective-permute-start | bytes 7077896 | tf_op jit(solution)/shard_map/cond/branch_2_fun/ppermute | solution.py:332
  45.6 32.3 %collective-permute-start.5 = (f32[3,1536,128]{2,1,0:T(8,128)}, f32[3,1536,128]{2,1,0:T(8,128)}, u32[]{:S(2)}, u32[]{:S(2)}) collective-permute-start(f32[3,1536,128]{2,1,0:T(8,128)} %get-tuple-element.87), channel_id=1, source_target_pairs={{1,0},{3,2},{4,3},{5,4},{7,6},{8,7},{9,8},{11,10},{12,11},{13,12},... | collective-permute-start | bytes 7077896 | tf_op jit(solution)/shard_map/cond/branch_2_fun/ppermute | solution.py:333
